TPU v7x, 1024 devices: a whole 8x8x8 slice. The times are simulated.
1024 devices in a mesh: pipe: 8 (over z), ctx: 128 (over y, x, core).
Axes of the slice: x: 8, y: 8, z: 8, core: 2. Of those that a mesh axis runs over, the one named last changes fastest.
Arguments:
- queries: bfloat16 [8, 16384, 4096], P('pipe', 'ctx'), may hold values from -6 to 6
- stash: bfloat16 [8, 16384, 1024], P('pipe', 'ctx'), may hold values from -6 to 6
- grad_out: bfloat16 [8, 16384, 4096], P('pipe', 'ctx'), may hold values from -6 to 6
- lengths: int32 [32], replicated, may hold values from 1 to 513, 16384 in all
Outputs:
- grad_kv: bfloat16 [8, 16384, 1024], P('pipe', 'ctx')
Inputs may be any that keep to these rules, and one draw needn't show every extreme that they name: The lengths sum to 16384; one document is exactly 513 long.
All inputs are finite; a program needn't handle non-finite values.
Results may differ from a plain program's by a relative error of at most 0.0059.
Values may be sent and summed in bfloat16 or wider, within the bound.
A program may use at most 32 MiB of HBM per device.

v0:
```python
import jax
import jax.numpy as jnp
from jax import lax
from jax.sharding import PartitionSpec as P

H = 32
KVH = 4
HD = 128
REACH = 5


def from_partner(block, axis, stride):
    count = lax.axis_size(axis)
    route = []
    for low in range(count):
        high = low | 1 << stride
        if high != low and high < count:
            route += [(low, high), (high, low)]
    return lax.ppermute(block, axis, route)


def from_behind(value, axis, steps):
    count = lax.axis_size(axis)
    first, last = (max(0, -steps), min(count, count - steps))
    return lax.ppermute(value, axis, [(source, source + steps) for source in range(first, last)])


def segment_of(positions, lengths):
    doc_ends = jnp.cumsum(lengths)
    return jnp.sum((doc_ends[None, :] <= positions[:, None]).astype(jnp.int32), axis=1)


def on_device(queries, stash, grad_out, lengths):
    row_count = queries.shape[1]
    group = H // KVH
    width_kv = 2 * KVH * HD
    high_bit = lax.axis_size("pipe").bit_length() - 2
    own_kv = from_partner(stash, "pipe", high_bit)[0]
    pieces = [own_kv]
    for back in range(1, REACH):
        pieces.insert(0, from_behind(own_kv, "ctx", back))
    joined = jnp.concatenate(pieces, axis=0)
    first_row = lax.axis_index("ctx") * row_count
    key_pos = first_row - (REACH - 1) * row_count + jnp.arange(REACH * row_count, dtype=jnp.int32)
    key_seg = segment_of(key_pos, lengths)
    tail = (REACH - 1) * row_count
    query_pos = key_pos[tail:]
    query_seg = key_seg[tail:]
    allowed = (
        (key_seg[None, :] == query_seg[:, None])
        & (key_pos[None, :] <= query_pos[:, None])
        & (key_pos[None, :] >= 0)
    )
    kv_heads = joined.reshape(REACH * row_count, 2, KVH, HD)
    keys_h = jnp.transpose(kv_heads[:, 0], (1, 0, 2))
    values_h = jnp.transpose(kv_heads[:, 1], (1, 0, 2))
    query_h = jnp.transpose(queries[0].reshape(row_count, KVH, group, HD), (1, 0, 2, 3))
    cot_h = jnp.transpose(grad_out[0].reshape(row_count, KVH, group, HD), (1, 0, 2, 3))
    score_scale = HD ** (-0.5)

    def head_grads(items):
        query_block, cotangent, key_block, value_block = items
        scores = (
            jnp.einsum("rgd,kd->grk", query_block, key_block, preferred_element_type=jnp.float32)
            * score_scale
        )
        scores = jnp.where(allowed[None], scores, -1e30)
        row_top = jnp.max(scores, axis=-1, keepdims=True)
        raw_weights = jnp.exp(scores - row_top)
        weights = raw_weights / jnp.sum(raw_weights, axis=-1, keepdims=True)
        weights16 = weights.astype(jnp.bfloat16)
        output = jnp.einsum(
            "grk,kd->rgd", weights16, value_block, preferred_element_type=jnp.float32
        )
        row_delta = jnp.sum(cotangent.astype(jnp.float32) * output, axis=-1)
        dweights = jnp.einsum(
            "rgd,kd->grk", cotangent, value_block, preferred_element_type=jnp.float32
        )
        dscores = (
            weights * (dweights - jnp.transpose(row_delta, (1, 0))[..., None]) * score_scale
        ).astype(jnp.bfloat16)
        grad_key = jnp.einsum(
            "grk,rgd->kd", dscores, query_block, preferred_element_type=jnp.float32
        )
        grad_value = jnp.einsum(
            "grk,rgd->kd", weights16, cotangent, preferred_element_type=jnp.float32
        )
        return (grad_key, grad_value)

    grad_key, grad_value = lax.map(head_grads, (query_h, cot_h, keys_h, values_h))
    key_grads = jnp.transpose(jnp.stack([grad_key, grad_value], axis=0), (2, 0, 1, 3))
    key_grads = key_grads.reshape(REACH, row_count, width_kv)
    total = key_grads[REACH - 1]
    for back in range(1, REACH):
        total = total + from_behind(key_grads[REACH - 1 - back], "ctx", -back)
    return total.astype(jnp.bfloat16).reshape(1, row_count, width_kv)


def solution(mesh):
    placed = (P("pipe", "ctx", None), P("pipe", "ctx", None), P("pipe", "ctx", None), P())
    return jax.shard_map(
        on_device, mesh=mesh, in_specs=placed, out_specs=P("pipe", "ctx", None), check_vma=False
    )
```

profile of v0, /device:TPU:444, one launch (start us, length us, event | category | flops | bytes accessed | tf_op | source)
XLA Modules:
  0.0 176.2 jit_solution(18146665839759665316)
XLA Ops:
  0.0 1.2 copy.27
  1.2 11.9 %collective-permute-start = (bf16[1,128,1024]{1,2,0:T(8,128)(2,1)S(1)}, bf16[1,128,1024]{1,2,0:T(8,128)(2,1)S(1)}, u32[]{:S(2)}, u32[]{:S(2)}) collective-permute-start(bf16[1,128,1024]{1,2,0:T(8,128)(2,1)S(1)} %copy.27), channel_id=1, source_target_pairs={{0,512},{512,0},{128,640},{640,128},{256,768},{768,256},{384,896},... | collective-permute-start | bytes 786440 | tf_op jit(solution)/shard_map/ppermute | solution.py:19
  13.1 11.9 %collective-permute-done = bf16[1,128,1024]{1,2,0:T(8,128)(2,1)S(1)} collective-permute-done((bf16[1,128,1024]{1,2,0:T(8,128)(2,1)S(1)}, bf16[1,128,1024]{1,2,0:T(8,128)(2,1)S(1)}, u32[]{:S(2)}, u32[]{:S(2)}) %collective-permute-start) | collective-permute-done | bytes 262176 | tf_op jit(solution)/shard_map/ppermute | solution.py:19
  25.0 4.6 %collective-permute-start.1 = (bf16[128,1024]{0,1:T(8,128)(2,1)S(1)}, bf16[128,1024]{0,1:T(8,128)(2,1)S(1)}, u32[]{:S(2)}, u32[]{:S(2)}) collective-permute-start(bf16[128,1024]{0,1:T(8,128)(2,1)S(1)} %bitcast.146), channel_id=1, source_target_pairs={{0,4},{1,5},{2,6},{3,7},{4,8},{5,9},{6,10},{7,11},{8,12},{9,13},{1... | collective-permute-start | bytes 786440 | tf_op jit(solution)/shard_map/ppermute | solution.py:25
  29.7 0.7 copy.30
  30.6 1.9 %collective-permute-start.2 = (bf16[128,1024]{0,1:T(8,128)(2,1)S(1)}, bf16[128,1024]{0,1:T(8,128)(2,1)S(1)}, u32[]{:S(2)}, u32[]{:S(2)}) collective-permute-start(bf16[128,1024]{0,1:T(8,128)(2,1)S(1)} %bitcast.147), channel_id=1, source_target_pairs={{0,3},{1,4},{2,5},{3,6},{4,7},{5,8},{6,9},{7,10},{8,11},{9,12},{10... | collective-permute-start | bytes 786440 | tf_op jit(solution)/shard_map/ppermute | solution.py:25
  32.6 3.4 %collective-permute-start.3 = (bf16[128,1024]{0,1:T(8,128)(2,1)S(1)}, bf16[128,1024]{0,1:T(8,128)(2,1)S(1)}, u32[]{:S(2)}, u32[]{:S(2)}) collective-permute-start(bf16[128,1024]{0,1:T(8,128)(2,1)S(1)} %bitcast.148), channel_id=1, source_target_pairs={{0,2},{1,3},{2,4},{3,5},{4,6},{5,7},{6,8},{7,9},{8,10},{9,11},{10,... | collective-permute-start | bytes 786440 | tf_op jit(solution)/shard_map/ppermute | solution.py:25
  36.1 1.6 copy.29
  37.7 1.3 copy.28
  39.0 4.1 %collective-permute-start.4 = (bf16[128,1024]{0,1:T(8,128)(2,1)S(1)}, bf16[128,1024]{0,1:T(8,128)(2,1)S(1)}, u32[]{:S(2)}, u32[]{:S(2)}) collective-permute-start(bf16[128,1024]{0,1:T(8,128)(2,1)S(1)} %bitcast.149), channel_id=1, source_target_pairs={{0,1},{1,2},{2,3},{3,4},{4,5},{5,6},{6,7},{7,8},{8,9},{9,10},{10,1... | collective-permute-start | bytes 786440 | tf_op jit(solution)/shard_map/ppermute | solution.py:25
  43.2 5.8 %collective-permute-done.2 = bf16[128,1024]{0,1:T(8,128)(2,1)S(1)} collective-permute-done((bf16[128,1024]{0,1:T(8,128)(2,1)S(1)}, bf16[128,1024]{0,1:T(8,128)(2,1)S(1)}, u32[]{:S(2)}, u32[]{:S(2)}) %collective-permute-start.2) | collective-permute-done | bytes 262176 | tf_op jit(solution)/shard_map/ppermute | solution.py:25
  49.1 5.9 %collective-permute-done.3 = bf16[128,1024]{0,1:T(8,128)(2,1)S(1)} collective-permute-done((bf16[128,1024]{0,1:T(8,128)(2,1)S(1)}, bf16[128,1024]{0,1:T(8,128)(2,1)S(1)}, u32[]{:S(2)}, u32[]{:S(2)}) %collective-permute-start.3) | collective-permute-done | bytes 262176 | tf_op jit(solution)/shard_map/ppermute | solution.py:25
  55.1 1.8 %collective-permute-done.4 = bf16[128,1024]{0,1:T(8,128)(2,1)S(1)} collective-permute-done((bf16[128,1024]{0,1:T(8,128)(2,1)S(1)}, bf16[128,1024]{0,1:T(8,128)(2,1)S(1)}, u32[]{:S(2)}, u32[]{:S(2)}) %collective-permute-start.4) | collective-permute-done | bytes 262176 | tf_op jit(solution)/shard_map/ppermute | solution.py:25
  57.0 1.0 slice_bitcast_fusion
  58.0 46.8 %while.13 = (s32[]{:T(128)}, f32[4,640,128]{2,1,0:T(8,128)}, f32[4,640,128]{2,1,0:T(8,128)}, bf16[4,640,128]{1,2,0:T(8,128)(2,1)}, bf16[4,128,8,128]{1,3,2,0:T(8...) while((s32[]{:T(128)}, f32[4,640,128]{2,1,0:T(8,128)}, ...), condition=%wide.region_6.7_spmd.clone, body=%wide.region_2.6_spmd.clone.sunk | while | flops 846790272 | bytes 15506293 | solution.py:90
  58.5 3.5 %fusion.88 = (f32[8,128]{1,0:T(8,128)S(1)}, f32[8,128,640]{1,2,0:T(8,128)}) fusion(pred[128,640]{0,1:T(8,128)(4,1)S(1)} %and_and_fusion.2, bf16[4,128,8,128]{1,3,2,0:T(8,128)(2,1)} %get-tuple-element.245, s32[]{:T(128)} %get-tuple-element.228, bf16[4,640,128]{1,2,0:T(8,128)(2,1)} %get-tuple-element.244), kind=kOutput, calls=%fused_computation.64.clone.1 | convolution fusion | flops 170394240 | bytes 3134464 | tf_op jit(solution)/shard_map/while/body/eval_jaxpr/sub | solution.py:69
  62.0 2.0 %fusion.89 = bf16[8,128,640]{1,2,0:T(8,128)(2,1)S(1)} fusion(f32[8,128,640]{1,2,0:T(8,128)} %get-tuple-element.213, f32[8,128]{1,0:T(8,128)S(1)} %get-tuple-element.214), kind=kLoop, calls=%fused_computation.23.clone.1 | loop fusion | flops 1310720 | bytes 3936256 | tf_op jit(solution)/shard_map/while/body/eval_jaxpr/convert_element_type | solution.py:71
  64.2 0.7 fusion.90
  64.9 3.5 %fusion.91 = f32[4,640,128]{2,1,0:T(8,128)} fusion(f32[4,640,128]{2,1,0:T(8,128)} %get-tuple-element.229, s32[]{:T(128)} %get-tuple-element.228, f32[8,128]{1,0:T(8,128)S(1)} %bitcast.155, f32[8,128,640]{1,2,0:T(8,128)} %get-tuple-element.213, f32[8,128]{1,0:T(8,128)S(1)} %get-tuple-element.214, bf16[4,128,8,128]{1,3,2,0:T(8,128)(2,1)} %get-tuple-element.245, ...), kind=kOutput, calls=%fused_computation.19.clone.1 | convolution fusion | flops 338821120 | bytes 3647488 | tf_op jit(solution)/shard_map/while/body/eval_jaxpr/grk,rgd->kd/dot_general | solution.py:82
  68.4 1.2 fusion.92
  70.2 3.5 %fusion.88 = (f32[8,128]{1,0:T(8,128)S(1)}, f32[8,128,640]{1,2,0:T(8,128)}) fusion(pred[128,640]{0,1:T(8,128)(4,1)S(1)} %and_and_fusion.2, bf16[4,128,8,128]{1,3,2,0:T(8,128)(2,1)} %get-tuple-element.245, s32[]{:T(128)} %get-tuple-element.228, bf16[4,640,128]{1,2,0:T(8,128)(2,1)} %get-tuple-element.244), kind=kOutput, calls=%fused_computation.64.clone.1 | convolution fusion | flops 170394240 | bytes 3134464 | tf_op jit(solution)/shard_map/while/body/eval_jaxpr/sub | solution.py:69
  73.7 2.0 %fusion.89 = bf16[8,128,640]{1,2,0:T(8,128)(2,1)S(1)} fusion(f32[8,128,640]{1,2,0:T(8,128)} %get-tuple-element.213, f32[8,128]{1,0:T(8,128)S(1)} %get-tuple-element.214), kind=kLoop, calls=%fused_computation.23.clone.1 | loop fusion | flops 1310720 | bytes 3936256 | tf_op jit(solution)/shard_map/while/body/eval_jaxpr/convert_element_type | solution.py:71
  75.9 0.7 fusion.90
  76.6 3.5 %fusion.91 = f32[4,640,128]{2,1,0:T(8,128)} fusion(f32[4,640,128]{2,1,0:T(8,128)} %get-tuple-element.229, s32[]{:T(128)} %get-tuple-element.228, f32[8,128]{1,0:T(8,128)S(1)} %bitcast.155, f32[8,128,640]{1,2,0:T(8,128)} %get-tuple-element.213, f32[8,128]{1,0:T(8,128)S(1)} %get-tuple-element.214, bf16[4,128,8,128]{1,3,2,0:T(8,128)(2,1)} %get-tuple-element.245, ...), kind=kOutput, calls=%fused_computation.19.clone.1 | convolution fusion | flops 338821120 | bytes 3647488 | tf_op jit(solution)/shard_map/while/body/eval_jaxpr/grk,rgd->kd/dot_general | solution.py:82
  80.1 1.2 fusion.92
  81.9 3.5 %fusion.88 = (f32[8,128]{1,0:T(8,128)S(1)}, f32[8,128,640]{1,2,0:T(8,128)}) fusion(pred[128,640]{0,1:T(8,128)(4,1)S(1)} %and_and_fusion.2, bf16[4,128,8,128]{1,3,2,0:T(8,128)(2,1)} %get-tuple-element.245, s32[]{:T(128)} %get-tuple-element.228, bf16[4,640,128]{1,2,0:T(8,128)(2,1)} %get-tuple-element.244), kind=kOutput, calls=%fused_computation.64.clone.1 | convolution fusion | flops 170394240 | bytes 3134464 | tf_op jit(solution)/shard_map/while/body/eval_jaxpr/sub | solution.py:69
  85.4 2.0 %fusion.89 = bf16[8,128,640]{1,2,0:T(8,128)(2,1)S(1)} fusion(f32[8,128,640]{1,2,0:T(8,128)} %get-tuple-element.213, f32[8,128]{1,0:T(8,128)S(1)} %get-tuple-element.214), kind=kLoop, calls=%fused_computation.23.clone.1 | loop fusion | flops 1310720 | bytes 3936256 | tf_op jit(solution)/shard_map/while/body/eval_jaxpr/convert_element_type | solution.py:71
  87.6 0.7 fusion.90
  88.3 3.5 %fusion.91 = f32[4,640,128]{2,1,0:T(8,128)} fusion(f32[4,640,128]{2,1,0:T(8,128)} %get-tuple-element.229, s32[]{:T(128)} %get-tuple-element.228, f32[8,128]{1,0:T(8,128)S(1)} %bitcast.155, f32[8,128,640]{1,2,0:T(8,128)} %get-tuple-element.213, f32[8,128]{1,0:T(8,128)S(1)} %get-tuple-element.214, bf16[4,128,8,128]{1,3,2,0:T(8,128)(2,1)} %get-tuple-element.245, ...), kind=kOutput, calls=%fused_computation.19.clone.1 | convolution fusion | flops 338821120 | bytes 3647488 | tf_op jit(solution)/shard_map/while/body/eval_jaxpr/grk,rgd->kd/dot_general | solution.py:82
  91.8 1.2 fusion.92
  93.6 3.5 %fusion.88 = (f32[8,128]{1,0:T(8,128)S(1)}, f32[8,128,640]{1,2,0:T(8,128)}) fusion(pred[128,640]{0,1:T(8,128)(4,1)S(1)} %and_and_fusion.2, bf16[4,128,8,128]{1,3,2,0:T(8,128)(2,1)} %get-tuple-element.245, s32[]{:T(128)} %get-tuple-element.228, bf16[4,640,128]{1,2,0:T(8,128)(2,1)} %get-tuple-element.244), kind=kOutput, calls=%fused_computation.64.clone.1 | convolution fusion | flops 170394240 | bytes 3134464 | tf_op jit(solution)/shard_map/while/body/eval_jaxpr/sub | solution.py:69
  97.1 2.0 %fusion.89 = bf16[8,128,640]{1,2,0:T(8,128)(2,1)S(1)} fusion(f32[8,128,640]{1,2,0:T(8,128)} %get-tuple-element.213, f32[8,128]{1,0:T(8,128)S(1)} %get-tuple-element.214), kind=kLoop, calls=%fused_computation.23.clone.1 | loop fusion | flops 1310720 | bytes 3936256 | tf_op jit(solution)/shard_map/while/body/eval_jaxpr/convert_element_type | solution.py:71
  99.3 0.7 fusion.90
  100.0 3.5 %fusion.91 = f32[4,640,128]{2,1,0:T(8,128)} fusion(f32[4,640,128]{2,1,0:T(8,128)} %get-tuple-element.229, s32[]{:T(128)} %get-tuple-element.228, f32[8,128]{1,0:T(8,128)S(1)} %bitcast.155, f32[8,128,640]{1,2,0:T(8,128)} %get-tuple-element.213, f32[8,128]{1,0:T(8,128)S(1)} %get-tuple-element.214, bf16[4,128,8,128]{1,3,2,0:T(8,128)(2,1)} %get-tuple-element.245, ...), kind=kOutput, calls=%fused_computation.19.clone.1 | convolution fusion | flops 338821120 | bytes 3647488 | tf_op jit(solution)/shard_map/while/body/eval_jaxpr/grk,rgd->kd/dot_general | solution.py:82
  103.5 1.2 fusion.92
  104.7 1.9 %maximum_bitcast_fusion = f32[640,2,4,128]{3,0,2,1:T(8,128)S(1)} fusion(f32[1,4,640,128]{3,2,1,0:T(8,128)} %bitcast.145, f32[1,4,640,128]{3,2,1,0:T(8,128)} %bitcast.144), kind=kLoop, calls=%fused_computation.51 | loop fusion | flops 655360 | bytes 5242880 | tf_op jit(solution)/shard_map/transpose | solution.py:91
  106.8 0.3 copy.36
  107.4 1.9 %collective-permute-start.5 = (f32[128,1024]{1,0:T(8,128)S(1)}, f32[128,1024]{1,0:T(8,128)}, u32[]{:S(2)}, u32[]{:S(2)}) collective-permute-start(f32[128,1024]{1,0:T(8,128)S(1)} %squeeze.42), channel_id=1, source_target_pairs={{1,0},{2,1},{3,2},{4,3},{5,4},{6,5},{7,6},{8,7},{9,8},{10,9},{11,1... | collective-permute-start | bytes 1572872 | tf_op jit(solution)/shard_map/ppermute | solution.py:25
  109.3 0.3 copy.37
  109.7 1.0 squeeze.43
  110.7 3.4 %collective-permute-start.6 = (f32[128,1024]{1,0:T(8,128)}, f32[128,1024]{1,0:T(8,128)}, u32[]{:S(2)}, u32[]{:S(2)}) collective-permute-start(f32[128,1024]{1,0:T(8,128)} %squeeze.43), channel_id=1, source_target_pairs={{2,0},{3,1},{4,2},{5,3},{6,4},{7,5},{8,6},{9,7},{10,8},{11,9},{12,... | collective-permute-start | bytes 1572872 | tf_op jit(solution)/shard_map/ppermute | solution.py:25
  114.1 0.3 copy.38
  114.7 5.1 %collective-permute-start.7 = (f32[128,1024]{1,0:T(8,128)S(1)}, f32[128,1024]{1,0:T(8,128)}, u32[]{:S(2)}, u32[]{:S(2)}) collective-permute-start(f32[128,1024]{1,0:T(8,128)S(1)} %squeeze.44), channel_id=1, source_target_pairs={{3,0},{4,1},{5,2},{6,3},{7,4},{8,5},{9,6},{10,7},{11,8},{12,9},{13... | collective-permute-start | bytes 1572872 | tf_op jit(solution)/shard_map/ppermute | solution.py:25
  120.4 2.1 %collective-permute-start.8 = (f32[128,1024]{1,0:T(8,128)S(1)}, f32[128,1024]{1,0:T(8,128)S(1)}, u32[]{:S(2)}, u32[]{:S(2)}) collective-permute-start(f32[128,1024]{1,0:T(8,128)S(1)} %squeeze.45), channel_id=1, source_target_pairs={{4,0},{5,1},{6,2},{7,3},{8,4},{9,5},{10,6},{11,7},{12,8},{13,9},{1... | collective-permute-start | bytes 1572872 | tf_op jit(solution)/shard_map/ppermute | solution.py:25
  123.0 8.8 %collective-permute-done.6 = f32[128,1024]{1,0:T(8,128)} collective-permute-done((f32[128,1024]{1,0:T(8,128)}, f32[128,1024]{1,0:T(8,128)}, u32[]{:S(2)}, u32[]{:S(2)}) %collective-permute-start.6) | collective-permute-done | bytes 524320 | tf_op jit(solution)/shard_map/ppermute | solution.py:25
  131.9 17.7 %collective-permute-done.7 = f32[128,1024]{1,0:T(8,128)} collective-permute-done((f32[128,1024]{1,0:T(8,128)S(1)}, f32[128,1024]{1,0:T(8,128)}, u32[]{:S(2)}, u32[]{:S(2)}) %collective-permute-start.7) | collective-permute-done | bytes 524320 | tf_op jit(solution)/shard_map/ppermute | solution.py:25
  149.6 24.4 %collective-permute-done.8 = f32[128,1024]{1,0:T(8,128)S(1)} collective-permute-done((f32[128,1024]{1,0:T(8,128)S(1)}, f32[128,1024]{1,0:T(8,128)S(1)}, u32[]{:S(2)}, u32[]{:S(2)}) %collective-permute-start.8) | collective-permute-done | bytes 524320 | tf_op jit(solution)/shard_map/ppermute | solution.py:25
  173.9 2.2 %fusion.56 = bf16[1,128,1024]{2,1,0:T(8,128)(2,1)} fusion(f32[128,1024]{1,0:T(8,128)S(1)} %collective-permute-done.8, f32[128,1024]{1,0:T(8,128)} %collective-permute-done.7, f32[128,1024]{1,0:T(8,128)} %collective-permute-done.6, f32[128,1024]{1,0:T(8,128)S(1)} %squeeze.41, f32[128,1024]{1,0:T(8,128)} %collective-permute-done.5), kind=kLoop, calls=%fused_computation.55 | loop fusion | flops 655360 | bytes 2883584 | tf_op jit(solution)/shard_map/reshape | solution.py:96
  (69 shorter events, 5.2 us)
Async XLA Ops:
  0.0 37.7 %copy-start = (bf16[1,128,4096]{2,1,0:T(8,128)(2,1)S(1)}, bf16[1,128,4096]{2,1,0:T(8,128)(2,1)}, u32[]{:S(2)}) copy-start(bf16[1,128,4096]{2,1,0:T(8,128)(2,1)} %param.6) | copy-start | bytes 3145732
  1.2 23.8 %collective-permute-start = (bf16[1,128,1024]{1,2,0:T(8,128)(2,1)S(1)}, bf16[1,128,1024]{1,2,0:T(8,128)(2,1)S(1)}, u32[]{:S(2)}, u32[]{:S(2)}) collective-permute-start(bf16[1,128,1024]{1,2,0:T(8,128)(2,1)S(1)} %copy.27), channel_id=1, source_target_pairs={{0,512},{512,0},{128,640},{640,128},{256,768},{768,256},{384,896},... | collective-permute-start | bytes 786440 | tf_op jit(solution)/shard_map/ppermute | solution.py:19
  25.0 18.1 %collective-permute-start.1 = (bf16[128,1024]{0,1:T(8,128)(2,1)S(1)}, bf16[128,1024]{0,1:T(8,128)(2,1)S(1)}, u32[]{:S(2)}, u32[]{:S(2)}) collective-permute-start(bf16[128,1024]{0,1:T(8,128)(2,1)S(1)} %bitcast.146), channel_id=1, source_target_pairs={{0,4},{1,5},{2,6},{3,7},{4,8},{5,9},{6,10},{7,11},{8,12},{9,13},{1... | collective-permute-start | bytes 786440 | tf_op jit(solution)/shard_map/ppermute | solution.py:25
  30.6 18.5 %collective-permute-start.2 = (bf16[128,1024]{0,1:T(8,128)(2,1)S(1)}, bf16[128,1024]{0,1:T(8,128)(2,1)S(1)}, u32[]{:S(2)}, u32[]{:S(2)}) collective-permute-start(bf16[128,1024]{0,1:T(8,128)(2,1)S(1)} %bitcast.147), channel_id=1, source_target_pairs={{0,3},{1,4},{2,5},{3,6},{4,7},{5,8},{6,9},{7,10},{8,11},{9,12},{10... | collective-permute-start | bytes 786440 | tf_op jit(solution)/shard_map/ppermute | solution.py:25
  32.6 22.4 %collective-permute-start.3 = (bf16[128,1024]{0,1:T(8,128)(2,1)S(1)}, bf16[128,1024]{0,1:T(8,128)(2,1)S(1)}, u32[]{:S(2)}, u32[]{:S(2)}) collective-permute-start(bf16[128,1024]{0,1:T(8,128)(2,1)S(1)} %bitcast.148), channel_id=1, source_target_pairs={{0,2},{1,3},{2,4},{3,5},{4,6},{5,7},{6,8},{7,9},{8,10},{9,11},{10,... | collective-permute-start | bytes 786440 | tf_op jit(solution)/shard_map/ppermute | solution.py:25
  39.0 17.8 %collective-permute-start.4 = (bf16[128,1024]{0,1:T(8,128)(2,1)S(1)}, bf16[128,1024]{0,1:T(8,128)(2,1)S(1)}, u32[]{:S(2)}, u32[]{:S(2)}) collective-permute-start(bf16[128,1024]{0,1:T(8,128)(2,1)S(1)} %bitcast.149), channel_id=1, source_target_pairs={{0,1},{1,2},{2,3},{3,4},{4,5},{5,6},{6,7},{7,8},{8,9},{9,10},{10,1... | collective-permute-start | bytes 786440 | tf_op jit(solution)/shard_map/ppermute | solution.py:25
  58.0 0.5 copy-start.1
  58.0 4.0 %copy-start.3 = (s32[128]{0:T(128)}, s32[128]{0:T(128)S(1)}, u32[]{:S(2)}) copy-start(s32[128]{0:T(128)S(1)} %get-tuple-element.248) | copy-start | bytes 1540 | tf_op jit(solution)/shard_map/while
  68.4 1.2 copy-start.2
  68.4 1.2 copy-start.4
  69.6 0.5 copy-start.1
  69.6 4.0 %copy-start.3 = (s32[128]{0:T(128)}, s32[128]{0:T(128)S(1)}, u32[]{:S(2)}) copy-start(s32[128]{0:T(128)S(1)} %get-tuple-element.248) | copy-start | bytes 1540 | tf_op jit(solution)/shard_map/while
  80.1 1.2 copy-start.2
  80.1 1.2 copy-start.4
  81.3 0.5 copy-start.1
  81.3 4.0 %copy-start.3 = (s32[128]{0:T(128)}, s32[128]{0:T(128)S(1)}, u32[]{:S(2)}) copy-start(s32[128]{0:T(128)S(1)} %get-tuple-element.248) | copy-start | bytes 1540 | tf_op jit(solution)/shard_map/while
  91.8 1.2 copy-start.2
  91.8 1.2 copy-start.4
  93.0 0.5 copy-start.1
  93.0 4.0 %copy-start.3 = (s32[128]{0:T(128)}, s32[128]{0:T(128)S(1)}, u32[]{:S(2)}) copy-start(s32[128]{0:T(128)S(1)} %get-tuple-element.248) | copy-start | bytes 1540 | tf_op jit(solution)/shard_map/while
  103.5 1.3 copy-start.2
  103.5 1.3 copy-start.4
  107.4 15.6 %collective-permute-start.5 = (f32[128,1024]{1,0:T(8,128)S(1)}, f32[128,1024]{1,0:T(8,128)}, u32[]{:S(2)}, u32[]{:S(2)}) collective-permute-start(f32[128,1024]{1,0:T(8,128)S(1)} %squeeze.42), channel_id=1, source_target_pairs={{1,0},{2,1},{3,2},{4,3},{5,4},{6,5},{7,6},{8,7},{9,8},{10,9},{11,1... | collective-permute-start | bytes 1572872 | tf_op jit(solution)/shard_map/ppermute | solution.py:25
  110.7 21.2 %collective-permute-start.6 = (f32[128,1024]{1,0:T(8,128)}, f32[128,1024]{1,0:T(8,128)}, u32[]{:S(2)}, u32[]{:S(2)}) collective-permute-start(f32[128,1024]{1,0:T(8,128)} %squeeze.43), channel_id=1, source_target_pairs={{2,0},{3,1},{4,2},{5,3},{6,4},{7,5},{8,6},{9,7},{10,8},{11,9},{12,... | collective-permute-start | bytes 1572872 | tf_op jit(solution)/shard_map/ppermute | solution.py:25
  114.7 34.9 %collective-permute-start.7 = (f32[128,1024]{1,0:T(8,128)S(1)}, f32[128,1024]{1,0:T(8,128)}, u32[]{:S(2)}, u32[]{:S(2)}) collective-permute-start(f32[128,1024]{1,0:T(8,128)S(1)} %squeeze.44), channel_id=1, source_target_pairs={{3,0},{4,1},{5,2},{6,3},{7,4},{8,5},{9,6},{10,7},{11,8},{12,9},{13... | collective-permute-start | bytes 1572872 | tf_op jit(solution)/shard_map/ppermute | solution.py:25
  120.4 53.6 %collective-permute-start.8 = (f32[128,1024]{1,0:T(8,128)S(1)}, f32[128,1024]{1,0:T(8,128)S(1)}, u32[]{:S(2)}, u32[]{:S(2)}) collective-permute-start(f32[128,1024]{1,0:T(8,128)S(1)} %squeeze.45), channel_id=1, source_target_pairs={{4,0},{5,1},{6,2},{7,3},{8,4},{9,5},{10,6},{11,7},{12,8},{13,9},{1... | collective-permute-start | bytes 1572872 | tf_op jit(solution)/shard_map/ppermute | solution.py:25
where the time goes:
time: 177 us; the launch traced here: 176 us
  waiting for transfers between devices  76.3 us (43%)
  starting transfers between devices  38.5 us (22%)
  matrix products  35.8 us (20%)
  other arithmetic  13.5 us (8%)
  local copies, waits for them, and re-layouts  11.6 us (7%)
    ppermute x8, waiting for transfers between devices, from_behind(): lax.ppermute(value, axis, [(source, source + steps) for source in range(f...  64.4 us
    ppermute x8, starting transfers between devices, from_behind(): lax.ppermute(value, axis, [(source, source + steps) for source in range(f...  26.6 us
    sub x4, matrix products, head_grads(): raw_weights = jnp.exp(scores - row_top)  14.1 us
    dot_general x4, matrix products, head_grads(): jnp.einsum('grk,rgd->kd', dscores, query_block, preferred_element_type=jn...  13.9 us
    ppermute x1, waiting for transfers between devices, from_partner(): return lax.ppermute(block, axis, route)  11.9 us
    ppermute x1, starting transfers between devices, from_partner(): return lax.ppermute(block, axis, route)  11.9 us
    convert_element_type x4, other arithmetic, head_grads(): weights16 = weights.astype(jnp.bfloat16)  7.83 us
    dot_general x4, matrix products, head_grads(): jnp.einsum('grk,rgd->kd', weights16, cotangent, preferred_element_type=jn...  4.93 us
  transfers between devices with their start and end apart: 9, of which 7 were waited for; matrix products, arithmetic and copies ran while one was open for 4% of the time, Pallas kernels for 0%

commit v1 on v0

v1 whole, which is shorter than its diff:
```python
import functools
import math

import jax
import jax.numpy as jnp
from jax import lax
from jax.experimental import pallas as pl
from jax.experimental.pallas import tpu as pltpu
from jax.sharding import PartitionSpec as P

MESH = pl.DeviceIdType.MESH
H = 32
KVH = 4
HD = 128
GROUP = H // KVH
ROWS = 128
TEAM = 4
OVER = 32
SPAN = TEAM * ROWS + 2 * OVER
RIGHT = SPAN - OVER
PAIR = 2 * ROWS
SCALE = HD**-0.5
LOG2E = math.log2(math.e)
FAR = 1 << 20


def block_rows(s):
    return pl.ds(OVER + s * ROWS, ROWS)


def dot_nt(a, b):
    return lax.dot_general(a, b, (((1,), (1,)), ((), ())), preferred_element_type=jnp.float32)


def dot_nn(a, b):
    return lax.dot_general(a, b, (((1,), (0,)), ((), ())), preferred_element_type=jnp.float32)


def add_terms(key, value, query, cot, lo, hi, acc, diag):
    rows = key.shape[0]
    raw = dot_nt(key, query)
    dprobs = dot_nt(value, cot)
    pos = lax.broadcasted_iota(jnp.int32, (rows, PAIR), 0)
    raw = jnp.where((pos >= lo) & (pos <= hi), raw, -1e30)
    top = jnp.maximum(jnp.max(raw, axis=0, keepdims=True), -1e29)
    weights = jnp.exp2((raw - top) * (SCALE * LOG2E))
    total = jnp.sum(weights, axis=0, keepdims=True)
    probs = weights * (1.0 / jnp.where(total > 0.0, total, 1.0))
    probs16 = probs.astype(jnp.bfloat16)
    delta = jnp.sum(probs16.astype(jnp.float32) * dprobs, axis=0, keepdims=True)
    dscores = (probs * (dprobs - delta) * SCALE).astype(jnp.bfloat16)
    acc[0, pl.ds(0, rows)] += dot_nn(dscores, query)
    acc[1, pl.ds(0, rows)] += dot_nn(probs16, cot)


def kernel(
    n_pipe, n_ctx, lengths, queries, stash, grad_out, out,
    mine, kv, q_own, c_own, q_over, c_over, acc, own, terms, got, got_left, got_right,
    load_sem, bulk_sem, zs, zr, fs, fr, os, orr, gs, gr, gl, gh,
):
    z, c = lax.axis_index("pipe"), lax.axis_index("ctx")
    team, j = c // TEAM, c % TEAM
    first = team * TEAM
    has_left, has_right = team > 0, team < n_ctx // TEAM - 1
    partner = (z ^ (n_pipe // 2), c)

    def at(offset):
        return (z, first + offset)

    def stash_loads():
        for h in range(KVH):
            for t in range(2):
                yield pltpu.make_async_copy(
                    stash.at[0, :, pl.ds((t * KVH + h) * HD, HD)], mine.at[h, t], load_sem.at[2 * h + t]
                )

    for copy in stash_loads():
        copy.start()

    barrier = pltpu.get_barrier_semaphore()

    def greet(device):
        pl.semaphore_signal(barrier, inc=1, device_id=device, device_id_type=MESH)

    greet(partner)
    for step in range(1, TEAM):
        greet(at((j + step) % TEAM))

    @pl.when(has_left)
    def _():
        greet(at(-1))

    @pl.when(has_left & (j == 0))
    def _():
        greet(at(-2))

    @pl.when(has_right & (j == 2))
    def _():
        greet(at(TEAM))

    @pl.when(has_right & (j == 3))
    def _():
        for other in range(TEAM):
            greet(at(TEAM + other))

    for head in range(H):
        columns = pl.ds(head * HD, HD)
        pltpu.make_async_copy(queries.at[0, :, columns], q_own.at[head], bulk_sem.at[0]).start()
        pltpu.make_async_copy(grad_out.at[0, :, columns], c_own.at[head], bulk_sem.at[1]).start()

    def prefix(i, carry):
        size = lengths[i]
        start, stop = carry
        return (start + jnp.where(i < team, size, 0), stop + jnp.where(i <= team, size, 0))

    base = first * ROWS - OVER
    start, stop = lax.fori_loop(0, lengths.shape[0], prefix, (jnp.int32(0), jnp.int32(0)))
    start, stop = start - base, stop - base

    @pl.when(jnp.logical_not(has_left))
    def _():
        for h in range(KVH):
            for t in range(2):
                kv[h, t, pl.ds(0, OVER), :] = jnp.zeros((OVER, HD), jnp.bfloat16)

    for copy in stash_loads():
        copy.wait()
    expected = 4 + jnp.where(has_left, jnp.where(j == 0, 2, 1), 0)
    expected += jnp.where(has_right, jnp.where(j == 2, 1, jnp.where(j == 3, 4, 0)), 0)
    pl.semaphore_wait(barrier, expected)

    def to_partner(h, t):
        return pltpu.make_async_remote_copy(
            mine.at[h, t], kv.at[h, t, pl.ds(OVER + j * ROWS, ROWS)], zs.at[2 * h + t], zr.at[2 * h + t],
            device_id=partner, device_id_type=MESH,
        )

    for h in range(KVH):
        for t in range(2):
            to_partner(h, t).start()

    pltpu.make_async_copy(q_own, q_own, bulk_sem.at[0]).wait()
    pltpu.make_async_copy(c_own, c_own, bulk_sem.at[1]).wait()

    def over_queries(device):
        head_rows = pl.ds(0, OVER)
        return [
            pltpu.make_async_remote_copy(
                own_ref.at[:, head_rows, :], over_ref, os.at[i], orr.at[i], device_id=device, device_id_type=MESH
            )
            for i, (own_ref, over_ref) in enumerate(((q_own, q_over), (c_own, c_over)))
        ]

    @pl.when(has_left & (j == 0))
    def _():
        for copy in over_queries(at(-2)):
            copy.start()

    def role(me):
        used = OVER + (me + 1) * ROWS

        near = {0: (3, 2, 1), 1: (3, 2), 2: (3,), 3: ()}[me]

        def forward(h, t, n, rows, there, device, slot):
            return pltpu.make_async_remote_copy(
                kv.at[h, t, rows], kv.at[h, t, there], fs.at[n, 2 * h + t], fr.at[slot, 2 * h + t],
                device_id=device, device_id_type=MESH,
            )

        def forwards(h, t, act):
            for n, other in enumerate(near):
                act(forward(h, t, n, block_rows(me), block_rows(me), at(other), me))
            if me == 0:

                @pl.when(has_left)
                def _():
                    act(forward(h, t, 3, pl.ds(OVER, OVER), pl.ds(RIGHT, OVER), at(-2), 5))

            if me == 3:

                @pl.when(has_right)
                def _():
                    act(forward(h, t, 0, block_rows(3), block_rows(3), at(2), 3))
                    for other in range(TEAM):
                        act(forward(h, t, 1 + other, pl.ds(RIGHT - OVER, OVER), pl.ds(0, OVER), at(TEAM + other), 4))

        def arrive(h, t):
            pltpu.make_async_remote_copy(
                mine.at[h, t], kv.at[h, t, block_rows(me)], zs.at[2 * h + t], zr.at[2 * h + t],
                device_id=partner, device_id_type=MESH,
            ).wait_recv()
            forwards(h, t, lambda copy: copy.start())

        def arrived(h, t, rows, slot):
            forward(h, t, 0, rows, rows, partner, slot).wait_recv()

        def term(h, n, rows, there, device, recv):
            return pltpu.make_async_remote_copy(
                terms.at[h, :, rows], there, gs.at[n, h], recv, device_id=device, device_id_type=MESH
            )

        def sent_terms(h, act):
            for s in range(me):
                act(term(h, s, block_rows(s), got.at[me - 1, h], at(s), gr.at[me - 1, h]))

            @pl.when(has_left)
            def _():
                act(term(h, 3, pl.ds(0, OVER), got_left.at[me, h], at(-1), gl.at[me, h]))

            if me == 2:

                @pl.when(has_right)
                def _():
                    act(term(h, 2, block_rows(3), got.at[1, h], at(3), gr.at[1, h]))
                    act(term(h, 4, pl.ds(RIGHT, OVER), got_right.at[h], at(TEAM), gh.at[h]))

        column = lax.broadcasted_iota(jnp.int32, (1, PAIR), 1)
        hi = OVER + me * ROWS + column % ROWS
        lo = jnp.where(hi >= stop, stop, jnp.where(hi >= start, start, FAR))

        def compute(h):
            for t in range(2):
                for s in range(me):
                    arrived(h, t, block_rows(s), s)

                @pl.when(has_left)
                def _():
                    arrived(h, t, pl.ds(0, OVER), 4)

            acc[...] = jnp.zeros_like(acc)

            def pair(p, _):
                heads = pl.ds(h * GROUP + 2 * p, 2)
                add_terms(
                    kv[h, 0, pl.ds(0, used)], kv[h, 1, pl.ds(0, used)],
                    q_own[heads].reshape(PAIR, HD), c_own[heads].reshape(PAIR, HD), lo, hi, acc, me,
                )
                return 0

            lax.fori_loop(0, GROUP // 2, pair, 0)
            if me == 2:

                @pl.when(has_right)
                def _():
                    for t in range(2):
                        arrived(h, t, block_rows(3), 3)
                        arrived(h, t, pl.ds(RIGHT, OVER), 5)
                    heads = pl.ds(h * GROUP, GROUP)
                    hi_over = RIGHT + column % OVER
                    lo_over = jnp.where(hi_over < stop, start, FAR)
                    add_terms(
                        kv[h, 0], kv[h, 1], q_over[heads].reshape(PAIR, HD), c_over[heads].reshape(PAIR, HD),
                        lo_over, hi_over, acc, 4,
                    )

            own[h] = acc[:, OVER + me * ROWS : OVER + (me + 1) * ROWS, :]
            terms[h] = acc[...].astype(jnp.bfloat16)
            sent_terms(h, lambda copy: copy.start())

        for t in range(2):
            arrive(0, t)
        if me == 2:

            @pl.when(has_right)
            def _():
                for copy in over_queries(at(TEAM)):
                    copy.wait_recv()

        def head_step(h, _):
            @pl.when(h < KVH - 1)
            def _():
                for t in range(2):
                    arrive(h + 1, t)

            compute(h)
            return 0

        lax.fori_loop(0, KVH, head_step, 0)

        for h in range(KVH):
            total = own[h]
            sources = {0: (1, 2, 3), 1: (2, 3), 2: (3,), 3: ()}[me]
            for source in sources:
                term(h, 0, block_rows(me), got.at[source - 1, h], partner, gr.at[source - 1, h]).wait_recv()
                total = total + got[source - 1, h].astype(jnp.float32)
            own[h] = total
            if me == 0:

                @pl.when(has_left)
                def _():
                    term(h, 0, pl.ds(0, OVER), got_right.at[h], partner, gh.at[h]).wait_recv()
                    own[h, :, pl.ds(0, OVER)] += got_right[h].astype(jnp.float32)

            if me == 3:

                @pl.when(has_right)
                def _():
                    term(h, 0, block_rows(me), got.at[1, h], partner, gr.at[1, h]).wait_recv()
                    own[h] += got[1, h].astype(jnp.float32)
                    for other in range(TEAM):
                        term(h, 0, pl.ds(0, OVER), got_left.at[other, h], partner, gl.at[other, h]).wait_recv()
                        own[h, :, pl.ds(ROWS - OVER, OVER)] += got_left[other, h].astype(jnp.float32)

            for t in range(2):
                out[0, :, (t * KVH + h) * HD : (t * KVH + h + 1) * HD] = own[h, t].astype(jnp.bfloat16)

        for h in range(KVH):
            for t in range(2):
                to_partner(h, t).wait_send()
                forwards(h, t, lambda copy: copy.wait_send())
            sent_terms(h, lambda copy: copy.wait_send())
        if me == 0:

            @pl.when(has_left)
            def _():
                for copy in over_queries(at(-2)):
                    copy.wait_send()

    for me in range(TEAM):
        pl.when(j == me)(functools.partial(role, me))


def on_device(n_pipe, n_ctx, queries, stash, grad_out, lengths):
    bf16, f32 = jnp.bfloat16, jnp.float32
    dma = pltpu.SemaphoreType.DMA
    anywhere = pl.BlockSpec(memory_space=pl.ANY)
    return pl.pallas_call(
        functools.partial(kernel, n_pipe, n_ctx),
        out_shape=jax.ShapeDtypeStruct((1, ROWS, 2 * KVH * HD), bf16),
        in_specs=[pl.BlockSpec(memory_space=pltpu.SMEM), anywhere, anywhere, anywhere],
        out_specs=pl.BlockSpec(memory_space=pltpu.VMEM),
        scratch_shapes=[
            pltpu.VMEM((KVH, 2, ROWS, HD), bf16),
            pltpu.VMEM((KVH, 2, SPAN, HD), bf16),
            pltpu.VMEM((H, ROWS, HD), bf16),
            pltpu.VMEM((H, ROWS, HD), bf16),
            pltpu.VMEM((H, OVER, HD), bf16),
            pltpu.VMEM((H, OVER, HD), bf16),
            pltpu.VMEM((2, SPAN, HD), f32),
            pltpu.VMEM((KVH, 2, ROWS, HD), f32),
            pltpu.VMEM((KVH, 2, SPAN, HD), bf16),
            pltpu.VMEM((TEAM - 1, KVH, 2, ROWS, HD), bf16),
            pltpu.VMEM((TEAM, KVH, 2, OVER, HD), bf16),
            pltpu.VMEM((KVH, 2, OVER, HD), bf16),
            dma((2 * KVH,)), dma((2,)), dma((2 * KVH,)), dma((2 * KVH,)), dma((5, 2 * KVH)), dma((6, 2 * KVH)),
            dma((2,)), dma((2,)), dma((5, KVH)), dma((3, KVH)), dma((TEAM, KVH)), dma((KVH,)),
        ],
        compiler_params=pltpu.CompilerParams(collective_id=0, has_side_effects=True, vmem_limit_bytes=48 << 20),
        name="document_backward",
    )(lengths, queries, stash, grad_out)


def solution(mesh):
    placed = (P("pipe", "ctx", None), P("pipe", "ctx", None), P("pipe", "ctx", None), P())
    body = functools.partial(on_device, mesh.shape["pipe"], mesh.shape["ctx"])
    return jax.shard_map(body, mesh=mesh, in_specs=placed, out_specs=P("pipe", "ctx", None), check_vma=False)
```

time: 177 us -> 55.3 us (0.31)
  the two profiles are of different devices: /device:TPU:444 before, /device:TPU:447 now
where the time goes in v1:
time: 55.3 us; the launch traced here: 55 us
  Pallas kernels  50.2 us (91%)
  local copies, waits for them, and re-layouts  4.76 us (9%)
    pallas_call x1, Pallas kernels, on_device(): pl.pallas_call(functools.partial(kernel, n_pipe, n_ctx), out_shape=jax.Sh...  50.2 us
    unnamed x9, local copies, waits for them, and re-layouts  4.76 us

profile of v1, /device:TPU:447, one launch (start us, length us, event | category | flops | bytes accessed | tf_op | source)
XLA Modules:
  0.0 55.0 jit_solution(2595766618431808532)
XLA Ops:
  0.0 0.0 copy-start
  0.0 1.2 %copy-done = bf16[1,128,4096]{2,1,0:T(8,128)(2,1)S(1)} copy-done((bf16[1,128,4096]{2,1,0:T(8,128)(2,1)S(1)}, bf16[1,128,4096]{2,1,0:T(8,128)(2,1)}, u32[]{:S(2)}) %copy-start) | copy-done | bytes 1048600
  1.2 0.0 copy-start.1
  1.2 1.2 %copy-done.1 = bf16[1,128,4096]{2,1,0:T(8,128)(2,1)S(1)} copy-done((bf16[1,128,4096]{2,1,0:T(8,128)(2,1)S(1)}, bf16[1,128,4096]{2,1,0:T(8,128)(2,1)}, u32[]{:S(2)}) %copy-start.1) | copy-done | bytes 1048600
  2.5 0.0 copy-start.2
  2.5 0.9 %copy-done.2 = bf16[1,128,1024]{2,1,0:T(8,128)(2,1)S(1)} copy-done((bf16[1,128,1024]{2,1,0:T(8,128)(2,1)S(1)}, bf16[1,128,1024]{2,1,0:T(8,128)(2,1)}, u32[]{:S(2)}) %copy-start.2) | copy-done | bytes 262168
  3.4 0.0 copy-start.3
  3.4 0.7 %copy-done.3 = s32[32]{0:T(128)S(1)} copy-done((s32[32]{0:T(128)S(1)}, s32[32]{0:T(128)}, u32[]{:S(2)}) %copy-start.3) | copy-done | bytes 152
  4.1 50.2 %document_backward.1 = bf16[1,128,1024]{2,1,0:T(8,128)(2,1)S(1)} custom-call(s32[32]{0:T(128)S(1)} %copy-done.3, bf16[1,128,4096]{2,1,0:T(8,128)(2,1)S(1)} %copy-done, bf16[1,128,1024]{2,1,0:T(8,128)(2,1)S(1)} %copy-done.2, bf16[1,128,4096]{2,1,0:T(8,128)(2,1)S(1)} %copy-done.1), custom_call_target="tpu_custom_call" | custom-call | tf_op jit(solution)/shard_map/document_backward/pallas_call | solution.py:327
  54.3 0.7 %copy.6 = bf16[1,128,1024]{2,1,0:T(8,128)(2,1)} copy(bf16[1,128,1024]{2,1,0:T(8,128)(2,1)S(1)} %document_backward.1) | data formatting | bytes 524288
Async XLA Ops:
  0.0 1.2 %copy-start = (bf16[1,128,4096]{2,1,0:T(8,128)(2,1)S(1)}, bf16[1,128,4096]{2,1,0:T(8,128)(2,1)}, u32[]{:S(2)}) copy-start(bf16[1,128,4096]{2,1,0:T(8,128)(2,1)} %queries.1) | copy-start | bytes 3145732
  1.2 1.2 %copy-start.1 = (bf16[1,128,4096]{2,1,0:T(8,128)(2,1)S(1)}, bf16[1,128,4096]{2,1,0:T(8,128)(2,1)}, u32[]{:S(2)}) copy-start(bf16[1,128,4096]{2,1,0:T(8,128)(2,1)} %grad_out.1) | copy-start | bytes 3145732
  2.5 0.9 %copy-start.2 = (bf16[1,128,1024]{2,1,0:T(8,128)(2,1)S(1)}, bf16[1,128,1024]{2,1,0:T(8,128)(2,1)}, u32[]{:S(2)}) copy-start(bf16[1,128,1024]{2,1,0:T(8,128)(2,1)} %stash.1) | copy-start | bytes 786436
  3.4 0.7 %copy-start.3 = (s32[32]{0:T(128)S(1)}, s32[32]{0:T(128)}, u32[]{:S(2)}) copy-start(s32[32]{0:T(128)} %lengths.1) | copy-start | bytes 388
